TPU v7x, 32 devices: a whole 2x2x4 slice. The times are simulated.
32 devices in a mesh: groups: 2 (over x), sample: 16 (over z, y, core).
Axes of the slice: x: 2, y: 2, z: 4, core: 2. Of those that a mesh axis runs over, the one named last changes fastest.
Arguments:
- prompt_states: bfloat16 [16384, 8192], P(('groups', 'sample')), parts along dimension 0, may hold values from -6 to 6
- page_table: int32 [128], P('groups'), parts along dimension 0, may hold values from 0 to 63, each once
- step_states: bfloat16 [2, 64, 8192], P(None, 'groups'), parts along dimension 1, may hold values from -15 to 15
- sample_order: int32 [64], P('groups'), parts along dimension 0, may hold values from 0 to 31, each once
- key_weight: bfloat16 [8192, 512], P('sample'), may hold values from -0.088388348 to 0.088388348
- value_weight: bfloat16 [8192, 512], P('sample'), may hold values from -0.0625 to 0.0625
- query_weight: bfloat16 [8192, 4096], P(None, 'sample'), may hold values from -0.121533978 to 0.121533978
- out_weight: bfloat16 [4096, 8192], P('sample'), may hold values from -0.125 to 0.125
Outputs:
- attn_out: bfloat16 [2, 64, 8192], P(None, 'groups', 'sample'), parts along dimension 1
There are 2 independent parts, one for each index of `groups`. A program takes and returns all parts, laid end to end along the dimension named above; an argument that names none is the same for every part. Nothing has to cross between parts.
Inputs may be any that keep to these rules, and one draw needn't show every extreme that they name: `page_table`: A permutation: entry p * 64 + j is the physical page that holds logical page j of prompt p; physical page r is rows r * 128 to (r + 1) * 128 - 1 of prompt_states. `sample_order`: A permutation; completion i continues prompt sample_order[i] // 32.
All inputs are finite; a program needn't handle non-finite values.
Results may differ from a plain program's by a relative error of at most 0.034.
Values may be sent and summed in bfloat16 or wider, within the bound.
A program may use at most 128 MiB of HBM per device.

v0:
```python
import jax
import jax.numpy as jnp
from jax import lax
from jax.sharding import PartitionSpec as P

D = 8192
HEAD_DIM = 128
KV_HEADS = 4
GQA = 8
PAGE = 128
PROMPT_PAGES = 64
rope_base = 1000000.0


def rotate(vector, position):
    half_dim = vector.shape[-1] // 2
    frequency = rope_base ** (-jnp.arange(half_dim, dtype=jnp.float32) * 2.0 / vector.shape[-1])
    angles = position.astype(jnp.float32)[..., None] * frequency
    cosine = jnp.cos(angles)
    sine_part = jnp.sin(angles)
    first_half = vector[..., :half_dim]
    second_half = vector[..., half_dim:]
    return jnp.concatenate(
        [
            first_half * cosine - second_half * sine_part,
            second_half * cosine + first_half * sine_part,
        ],
        axis=-1,
    )


def finish_heads(prefix_top, prefix_total, prefix_sum, queries, new_keys, new_values):
    score_scale = queries.shape[-1] ** (-0.5)
    query_wide = queries.astype(jnp.float32)
    key_wide = new_keys.astype(jnp.float32)
    value_wide = new_values.astype(jnp.float32)
    own_score = jnp.sum(query_wide * key_wide, axis=-1) * score_scale
    back_score = jnp.sum(query_wide[1] * key_wide[0], axis=-1) * score_scale
    first_high = jnp.maximum(prefix_top[0], own_score[0])
    first_old = jnp.exp(prefix_top[0] - first_high)
    first_own = jnp.exp(own_score[0] - first_high)
    first_out = (first_old[..., None] * prefix_sum[0] + first_own[..., None] * value_wide[0]) / (
        first_old * prefix_total[0] + first_own
    )[..., None]
    second_high = jnp.maximum(jnp.maximum(prefix_top[1], own_score[1]), back_score)
    second_old = jnp.exp(prefix_top[1] - second_high)
    second_back = jnp.exp(back_score - second_high)
    second_own = jnp.exp(own_score[1] - second_high)
    second_num = (
        second_old[..., None] * prefix_sum[1]
        + second_back[..., None] * value_wide[0]
        + second_own[..., None] * value_wide[1]
    )
    second_out = second_num / (second_old * prefix_total[1] + second_back + second_own)[..., None]
    return jnp.stack([first_out, second_out]).astype(jnp.bfloat16)


def on_device(
    prompt_states,
    page_table,
    step_states,
    sample_order,
    key_weight,
    value_weight,
    query_weight,
    out_weight,
):
    devices = lax.axis_size("sample")
    own_index = lax.axis_index("sample")
    row_count = prompt_states.shape[0]
    pages_here = row_count // PAGE
    heads_here = query_weight.shape[1] // HEAD_DIM
    total_pages = page_table.shape[0]
    prompts = total_pages // PROMPT_PAGES
    samples = sample_order.shape[0]
    group_size = samples // prompts
    score_scale = HEAD_DIM ** (-0.5)
    own_kv = own_index * heads_here // GQA
    slot_of = (
        jnp.zeros((total_pages,), jnp.int32)
        .at[page_table]
        .set(jnp.arange(total_pages, dtype=jnp.int32))
    )
    local_slots = lax.dynamic_slice_in_dim(slot_of, own_index * pages_here, pages_here)
    positions = (local_slots % PROMPT_PAGES * PAGE)[:, None] + jnp.arange(PAGE, dtype=jnp.int32)[
        None, :
    ]
    positions = positions.reshape(row_count)
    wide_states = step_states.reshape(2 * samples, D)
    key_piece = lax.all_gather(key_weight, "sample", axis=0, tiled=True)
    value_piece = lax.all_gather(value_weight, "sample", axis=0, tiled=True)
    piece_rows = key_piece.shape[0]
    key_acc = jnp.einsum(
        "rn,nkd->krd",
        prompt_states,
        key_piece.reshape(piece_rows, KV_HEADS, HEAD_DIM),
        preferred_element_type=jnp.float32,
    )
    value_acc = jnp.einsum(
        "rn,nkd->krd",
        prompt_states,
        value_piece.reshape(piece_rows, KV_HEADS, HEAD_DIM),
        preferred_element_type=jnp.float32,
    )
    key_head = lax.dynamic_slice_in_dim(key_piece, own_kv * HEAD_DIM, HEAD_DIM, 1)
    value_head = lax.dynamic_slice_in_dim(value_piece, own_kv * HEAD_DIM, HEAD_DIM, 1)
    key_step = jnp.dot(wide_states, key_head, preferred_element_type=jnp.float32)
    value_step = jnp.dot(wide_states, value_head, preferred_element_type=jnp.float32)
    key_acc, value_acc, key_step, value_step = (key_acc, value_acc, key_step, value_step)
    page_keys = rotate(key_acc, positions[None, :]).astype(jnp.bfloat16)
    page_values = value_acc.astype(jnp.bfloat16)
    step_place = (PROMPT_PAGES * PAGE + jnp.arange(2, dtype=jnp.int32))[:, None, None]
    queries = jnp.dot(wide_states, query_weight, preferred_element_type=jnp.float32).reshape(
        2, samples, heads_here, HEAD_DIM
    )
    queries = rotate(queries, step_place).astype(jnp.bfloat16)
    new_keys = rotate(key_step.reshape(2, samples, HEAD_DIM), step_place[:, :, 0]).astype(
        jnp.bfloat16
    )
    new_values = value_step.reshape(2, samples, HEAD_DIM).astype(jnp.bfloat16)
    inverse = (
        jnp.zeros((samples,), jnp.int32).at[sample_order].set(jnp.arange(samples, dtype=jnp.int32))
    )
    spread = devices // KV_HEADS
    send_keys = jnp.repeat(page_keys, spread, axis=0)
    send_values = jnp.repeat(page_values, spread, axis=0)
    all_keys, all_values = (
        lax.all_to_all(send_keys, "sample", split_axis=0, concat_axis=1, tiled=True),
        lax.all_to_all(send_values, "sample", split_axis=0, concat_axis=1, tiled=True),
    )
    logical = page_table.reshape(prompts, PROMPT_PAGES)
    all_keys = all_keys.reshape(total_pages, PAGE, HEAD_DIM)[logical].reshape(
        prompts, PROMPT_PAGES * PAGE, HEAD_DIM
    )
    all_values = all_values.reshape(total_pages, PAGE, HEAD_DIM)[logical].reshape(
        prompts, PROMPT_PAGES * PAGE, HEAD_DIM
    )
    sorted_query = queries[:, inverse].reshape(2, prompts, group_size, heads_here, HEAD_DIM)
    scores = (
        jnp.einsum("spmhd,pld->spmhl", sorted_query, all_keys, preferred_element_type=jnp.float32)
        * score_scale
    )
    prefix_top = jnp.max(scores, axis=-1)
    weights = jnp.exp(scores - prefix_top[..., None])
    prefix_total = jnp.sum(weights, axis=-1)
    prefix_sum = jnp.einsum(
        "spmhl,pld->spmhd",
        weights.astype(jnp.bfloat16),
        all_values,
        preferred_element_type=jnp.float32,
    )
    prefix_top = prefix_top.reshape(2, samples, heads_here)[:, sample_order]
    prefix_total = prefix_total.reshape(2, samples, heads_here)[:, sample_order]
    prefix_sum = prefix_sum.reshape(2, samples, heads_here, HEAD_DIM)[:, sample_order]
    head_out = finish_heads(
        prefix_top,
        prefix_total,
        prefix_sum,
        queries,
        new_keys[:, :, None, :],
        new_values[:, :, None, :],
    )
    flat_heads = head_out.reshape(2, samples, heads_here * HEAD_DIM)
    head_terms = jnp.einsum(
        "srk,kd->srd", flat_heads, out_weight, preferred_element_type=jnp.float32
    )
    return lax.psum_scatter(
        head_terms.astype(jnp.bfloat16), "sample", scatter_dimension=2, tiled=True
    )


def solution(mesh):
    in_specs = (
        P(("groups", "sample"), None),
        P("groups"),
        P(None, "groups", None),
        P("groups"),
        P("sample", None),
        P("sample", None),
        P(None, "sample"),
        P("sample", None),
    )
    out_specs = P(None, "groups", "sample")
    return jax.shard_map(
        on_device, mesh=mesh, in_specs=in_specs, out_specs=out_specs, check_vma=False
    )
```

profile of v0, /device:TPU:0, one launch (start us, length us, event | category | flops | bytes accessed | tf_op | source)
XLA Modules:
  0.0 351.2 jit_solution(6273337491218514646)
XLA Ops:
  10.2 77.0 %all-gather.3.cloned.1.call-done = bf16[8192,512]{1,0:T(8,128)(2,1)} async-done(((bf16[512,512]{1,0:T(8,128)(2,1)}), bf16[8192,512]{1,0:T(8,128)(2,1)}) %all-gather.3.cloned.1.call-update) | async-done | bytes 8388624 | tf_op jit(solution)/shard_map/all_gather | solution.py:90
  87.2 11.5 %copy.36 = bf16[8192,512]{0,1:T(8,128)(2,1)} copy(bf16[8192,512]{1,0:T(8,128)(2,1)} %all-gather.3.cloned.1.call-done) | data formatting | bytes 16777216 | tf_op jit(solution)/shard_map/all_gather | solution.py:90
  98.6 9.5 %fusion.16 = f32[4,512,128]{1,2,0:T(8,128)S(1)} fusion(bf16[8192,4,128]{0,2,1:T(8,128)(2,1)} %bitcast.153, bf16[512,8192]{1,0:T(8,128)(2,1)} %param.8), kind=kOutput, calls=%fused_computation.26 | convolution fusion | flops 4294967296 | bytes 17825792 | tf_op jit(solution)/shard_map/rn,nkd->krd/dot_general | solution.py:93
  108.7 1.8 broadcast_in_dim.13
  110.5 3.7 %all-to-all-start = ((bf16[16,512,128]{2,1,0:T(8,128)(2,1)}), bf16[16,512,128]{2,1,0:T(8,128)(2,1)S(1)}, u32[]{:S(2)}, u32[]{:S(2)}) async-start(bf16[16,512,128]{2,1,0:T(8,128)(2,1)} %bitcast.4), calls=%async_computation | async-start | bytes 4194304 | tf_op jit(solution)/shard_map/all_to_all | solution.py:128
  114.2 6.4 %copy.61 = bf16[256,8192]{1,0:T(8,128)(2,1)} copy(bf16[256,8192]{0,1:T(8,128)(2,1)} %bitcast.158) | data formatting | bytes 8388608 | tf_op jit(solution)/shard_map/dot_general | solution.py:113
  120.7 4.3 %fusion.37 = f32[2,32,2,128]{3,1,2,0:T(8,128)S(1)} fusion(bf16[2,128,8192,1]{2,1,0,3:T(8,128)(2,1)} %bitcast.152, bf16[2,32,8192]{2,1,0:T(8,128)(2,1)S(1)} %copy-done), kind=kOutput, calls=%fused_computation.33 | convolution fusion | flops 268435456 | bytes 5308416 | tf_op jit(solution)/shard_map/dot_general | solution.py:113
  125.1 69.1 %all-gather.5.cloned.1.call-done = bf16[8192,512]{1,0:T(8,128)(2,1)} async-done(((bf16[512,512]{1,0:T(8,128)(2,1)}), bf16[8192,512]{1,0:T(8,128)(2,1)}) %all-gather.5.cloned.1.call-update) | async-done | bytes 8388624 | tf_op jit(solution)/shard_map/all_gather | solution.py:91
  194.2 11.4 %copy.44 = bf16[8192,512]{0,1:T(8,128)(2,1)} copy(bf16[8192,512]{1,0:T(8,128)(2,1)} %all-gather.5.cloned.1.call-done) | data formatting | bytes 16777216 | tf_op jit(solution)/shard_map/all_gather | solution.py:91
  205.6 11.1 %fusion.22 = bf16[4,512,128]{1,2,0:T(8,128)(2,1)} fusion(bf16[8192,4,128]{0,2,1:T(8,128)(2,1)} %bitcast.154, bf16[512,8192]{1,0:T(8,128)(2,1)} %param.8), kind=kOutput, calls=%fused_computation.28 | convolution fusion | flops 4295229440 | bytes 17301504 | tf_op jit(solution)/shard_map/rn,nkd->krd/dot_general | solution.py:99
  216.7 2.1 copy.45
  218.7 2.8 broadcast_in_dim.17
  221.6 7.3 %all-to-all-start.1 = ((bf16[16,512,128]{2,1,0:T(8,128)(2,1)}), bf16[16,512,128]{2,1,0:T(8,128)(2,1)}, u32[]{:S(2)}, u32[]{:S(2)}) async-start(bf16[16,512,128]{2,1,0:T(8,128)(2,1)} %bitcast.26), calls=%async_computation.1 | async-start | bytes 4194304 | tf_op jit(solution)/shard_map/all_to_all | solution.py:129
  229.2 0.9 scatter_custom_fusion.1
  230.7 2.1 fusion.14
  233.3 2.1 fusion.34
  235.4 2.1 gather_fusion
  237.5 4.2 %fusion.77 = (f32[2,32,2]{1,2,0:T(2,128)S(1)}, f32[2,1,32,2,8192]{4,2,3,0,1:T(8,128)}) fusion(bf16[8192,128,1,1]{1,0,3,2:T(8,128)(2,1)} %bitcast.156, bf16[2,32,2,128]{3,2,0,1:T(2,128)(2,1)S(1)} %bitcast.163), kind=kOutput, calls=%fused_computation.111 | convolution fusion | flops 270532480 | bytes 6324736 | tf_op jit(solution)/shard_map/spmhd,pld->spmhl/dot_general | solution.py:140
  241.9 2.9 fusion.6
  247.1 22.9 %all-to-all-done.1 = bf16[16,512,128]{2,1,0:T(8,128)(2,1)} async-done(((bf16[16,512,128]{2,1,0:T(8,128)(2,1)}), bf16[16,512,128]{2,1,0:T(8,128)(2,1)}, u32[]{:S(2)}, u32[]{:S(2)}) %all-to-all-start.1) | async-done | bytes 2097184 | tf_op jit(solution)/shard_map/all_to_all | solution.py:129
  270.0 2.5 gather_fusion.3
  272.6 3.0 fusion.25
  276.7 4.0 %convolution_convert_fusion = bf16[2,32,8192]{2,1,0:T(8,128)(2,1)} fusion(bf16[256,8192]{1,0:T(8,128)(2,1)} %param.15, bf16[1,32,256]{2,1,0:T(8,128)(2,1)S(1)} %stack.10, bf16[1,32,256]{2,1,0:T(8,128)(2,1)S(1)} %stack.9), kind=kOutput, calls=%fused_computation.10 | convolution fusion | flops 268976128 | bytes 5275648 | tf_op jit(solution)/shard_map/srk,kd->srd/dot_general | solution.py:164
  280.7 64.0 %reduce-scatter.2.cloned.1.call-done = bf16[2,32,512]{2,1,0:T(8,128)(2,1)} async-done(((bf16[2,32,8192]{2,1,0:T(8,128)(2,1)}), bf16[2,32,512]{2,1,0:T(8,128)(2,1)}) %reduce-scatter.2.cloned.1.call-update) | async-done | bytes 65552 | tf_op jit(solution)/shard_map/reduce_scatter | solution.py:167
  (63 shorter events, 9.0 us)
Async XLA Ops:
  6.5 114.2 %copy-start = (bf16[2,32,8192]{2,1,0:T(8,128)(2,1)S(1)}, bf16[2,32,8192]{2,1,0:T(8,128)(2,1)}, u32[]{:S(2)}) copy-start(bf16[2,32,8192]{2,1,0:T(8,128)(2,1)} %param.10) | copy-start | bytes 3145732
  6.5 80.6 %all-gather.3.cloned.1.call-start = ((), (), s32[]{:S(2)}) async-start(), calls=%async_computation.3 | async-start | bytes 8912896 | tf_op jit(solution)/shard_map/all_gather | solution.py:90
  7.3 186.9 %all-gather.5.cloned.1.call-start = ((), (), s32[]{:S(2)}) async-start(), calls=%async_computation.4 | async-start | bytes 8912896 | tf_op jit(solution)/shard_map/all_gather | solution.py:91
  110.5 108.3 %all-to-all-start = ((bf16[16,512,128]{2,1,0:T(8,128)(2,1)}), bf16[16,512,128]{2,1,0:T(8,128)(2,1)S(1)}, u32[]{:S(2)}, u32[]{:S(2)}) async-start(bf16[16,512,128]{2,1,0:T(8,128)(2,1)} %bitcast.4), calls=%async_computation | async-start | bytes 4194304 | tf_op jit(solution)/shard_map/all_to_all | solution.py:128
  216.7 12.5 %copy-start.1 = (s32[32]{0:T(128)S(1)}, s32[32]{0:T(128)}, u32[]{:S(2)}) copy-start(s32[32]{0:T(128)} %param.11) | copy-start | bytes 388
  221.6 48.4 %all-to-all-start.1 = ((bf16[16,512,128]{2,1,0:T(8,128)(2,1)}), bf16[16,512,128]{2,1,0:T(8,128)(2,1)}, u32[]{:S(2)}, u32[]{:S(2)}) async-start(bf16[16,512,128]{2,1,0:T(8,128)(2,1)} %bitcast.26), calls=%async_computation.1 | async-start | bytes 4194304 | tf_op jit(solution)/shard_map/all_to_all | solution.py:129
  228.9 115.8 %reduce-scatter.2.cloned.1.call-start = ((), (), s32[]{:S(2)}) async-start(), calls=%async_computation.5 | async-start | bytes 1114112 | tf_op jit(solution)/shard_map/reduce_scatter | solution.py:167
Sparse Core Ops, SparseCore 0:
  9.5 77.5 all-gather.2
  89.3 104.7 all-gather.4
  280.8 63.8 reduce-scatter.1
where the time goes:
time: 352 us; the launch traced here: 351 us
  waiting for transfers between devices  234 us (66%)
  local copies, waits for them, and re-layouts  46.4 us (13%)
  matrix products  40.4 us (11%)
  between operations  13.4 us (4%)
  starting transfers between devices  11.1 us (3%)
  other arithmetic  5.57 us (2%)
    all_gather x1, waiting for transfers between devices, on_device(): key_piece = lax.all_gather(key_weight, 'sample', axis=0, tiled=True)  77 us
    all_gather x1, waiting for transfers between devices, on_device(): value_piece = lax.all_gather(value_weight, 'sample', axis=0, tiled=True)  69.1 us
    reduce_scatter x1, waiting for transfers between devices, on_device(): lax.psum_scatter(head_terms.astype(jnp.bfloat16), 'sample', scatter_dimen...  64 us
    all_to_all x1, waiting for transfers between devices, on_device(): lax.all_to_all(send_values, 'sample', split_axis=0, concat_axis=1, tiled=...  22.9 us
    all_gather x1, local copies, waits for them, and re-layouts, on_device(): key_piece = lax.all_gather(key_weight, 'sample', axis=0, tiled=True)  11.5 us
    all_gather x1, local copies, waits for them, and re-layouts, on_device(): value_piece = lax.all_gather(value_weight, 'sample', axis=0, tiled=True)  11.4 us
    dot_general x1, matrix products, on_device(): jnp.einsum('rn,nkd->krd', prompt_states, value_piece.reshape(piece_rows,...  11.1 us
    dot_general x1, matrix products, on_device(): jnp.einsum('rn,nkd->krd', prompt_states, key_piece.reshape(piece_rows, KV...  9.54 us
  transfers between devices with their start and end apart: 5, of which 4 were waited for; matrix products, arithmetic and copies ran while one was open for 22% of the time, Pallas kernels for 0%

commit v1 on v0

--- a/solution.py
+++ b/solution.py
@@ -87,8 +87,13 @@
     ]
     positions = positions.reshape(row_count)
     wide_states = step_states.reshape(2 * samples, D)
-    key_piece = lax.all_gather(key_weight, "sample", axis=0, tiled=True)
-    value_piece = lax.all_gather(value_weight, "sample", axis=0, tiled=True)
+    key_piece, value_piece = jnp.split(
+        lax.all_gather(
+            jnp.concatenate([key_weight, value_weight], axis=1), "sample", axis=0, tiled=True
+        ),
+        [key_weight.shape[1]],
+        axis=1,
+    )
     piece_rows = key_piece.shape[0]
     key_acc = jnp.einsum(
         "rn,nkd->krd",

time: 352 us -> 365 us (1.037)
  local copies, waits for them, and re-layouts: 46.4 us -> 58 us
  starting transfers between devices: 11.1 us -> 15 us
  matrix products: 40.4 us -> 36.7 us
    split x0 -> x3, local copies, waits for them, and re-layouts: none -> 34.1 us  [on_device(): jnp.split(lax.all_gather(jnp.concatenate([key_weight, value_weight], axis...]
    all_gather x2 -> x0, local copies, waits for them, and re-layouts: 22.9 us -> none  [the longest x1 11.5 us: on_device(): key_piece = lax.all_gather(key_weight, 'sample', axis=0, tiled=True)]
    all_to_all x1, waiting for transfers between devices: 0.01 us -> 22.3 us  [on_device(): lax.all_to_all(send_keys, 'sample', split_axis=0, concat_axis=1, tiled=True)]
    all_gather x2 -> x1, waiting for transfers between devices: 146 us -> 130 us  [on_device(): lax.all_gather(jnp.concatenate([key_weight, value_weight], axis=1), 'samp...]
    all_to_all x1, starting transfers between devices: 3.72 us -> 11.2 us  [on_device(): lax.all_to_all(send_keys, 'sample', split_axis=0, concat_axis=1, tiled=True)]
    all_to_all x1, waiting for transfers between devices: 22.9 us -> 15.5 us  [on_device(): lax.all_to_all(send_values, 'sample', split_axis=0, concat_axis=1, tiled=...]
  transfers between devices with their start and end apart: 5 -> 4, of which waited for: 4 -> 4; matrix products, arithmetic and copies ran while one was open for 22% -> 12% of each run, Pallas kernels for 0% -> 0%
where the time goes in v1:
time: 365 us; the launch traced here: 364 us
  waiting for transfers between devices  232 us (64%)
  local copies, waits for them, and re-layouts  58 us (16%)
  matrix products  36.7 us (10%)
  starting transfers between devices  15 us (4%)
  between operations  13.7 us (4%)
  other arithmetic  8.25 us (2%)
    all_gather x1, waiting for transfers between devices, on_device(): lax.all_gather(jnp.concatenate([key_weight, value_weight], axis=1), 'samp...  130 us
    reduce_scatter x1, waiting for transfers between devices, on_device(): lax.psum_scatter(head_terms.astype(jnp.bfloat16), 'sample', scatter_dimen...  64 us
    split x3, local copies, waits for them, and re-layouts, on_device(): jnp.split(lax.all_gather(jnp.concatenate([key_weight, value_weight], axis...  34.1 us
    all_to_all x1, waiting for transfers between devices, on_device(): lax.all_to_all(send_keys, 'sample', split_axis=0, concat_axis=1, tiled=True)  22.3 us
    all_to_all x1, waiting for transfers between devices, on_device(): lax.all_to_all(send_values, 'sample', split_axis=0, concat_axis=1, tiled=...  15.5 us
    all_to_all x1, starting transfers between devices, on_device(): lax.all_to_all(send_keys, 'sample', split_axis=0, concat_axis=1, tiled=True)  11.2 us
    dot_general x1, matrix products, on_device(): jnp.einsum('rn,nkd->krd', prompt_states, value_piece.reshape(piece_rows,...  10.3 us
    dot_general x1, matrix products, on_device(): jnp.einsum('rn,nkd->krd', prompt_states, key_piece.reshape(piece_rows, KV...  9.51 us
  transfers between devices with their start and end apart: 4, of which 4 were waited for; matrix products, arithmetic and copies ran while one was open for 12% of the time, Pallas kernels for 0%

profile of v1, /device:TPU:0, one launch (start us, length us, event | category | flops | bytes accessed | tf_op | source)
XLA Modules:
  0.0 363.7 jit_solution(5632403991931673837)
XLA Ops:
  6.5 2.4 pad_maximum_fusion
  8.9 130.2 %all-gather.2.cloned.1.call-done = bf16[8192,1024]{1,0:T(8,128)(2,1)} async-done(((bf16[512,1024]{1,0:T(8,128)(2,1)}), bf16[8192,1024]{1,0:T(8,128)(2,1)}) %all-gather.2.cloned.1.call-update) | async-done | bytes 16777232 | tf_op jit(solution)/shard_map/all_gather | solution.py:91
  139.1 11.3 %fusion.74 = (bf16[8192,512]{1,0:T(8,128)(2,1)}, bf16[8192,512]{1,0:T(8,128)(2,1)}) fusion(bf16[8192,1024]{1,0:T(8,128)(2,1)} %all-gather.2.cloned.1.call-done), kind=kLoop, calls=%fused_computation.109 | loop fusion | bytes 33554432 | tf_op jit(solution)/shard_map/split | solution.py:90
  150.4 11.4 %copy.44 = bf16[8192,512]{0,1:T(8,128)(2,1)} copy(bf16[8192,512]{1,0:T(8,128)(2,1)} %get-tuple-element.15) | data formatting | bytes 16777216 | tf_op jit(solution)/shard_map/split | solution.py:90
  161.8 10.3 %fusion.22 = bf16[4,512,128]{1,2,0:T(8,128)(2,1)S(1)} fusion(bf16[8192,4,128]{0,2,1:T(8,128)(2,1)} %bitcast.153, bf16[512,8192]{1,0:T(8,128)(2,1)} %param.8), kind=kOutput, calls=%fused_computation.28 | convolution fusion | flops 4295229440 | bytes 17301504 | tf_op jit(solution)/shard_map/rn,nkd->krd/dot_general | solution.py:104
  174.2 3.7 %all-to-all-start.1 = ((bf16[16,512,128]{2,1,0:T(8,128)(2,1)}), bf16[16,512,128]{2,1,0:T(8,128)(2,1)S(1)}, u32[]{:S(2)}, u32[]{:S(2)}) async-start(bf16[16,512,128]{2,1,0:T(8,128)(2,1)} %bitcast.26), calls=%async_computation.1 | async-start | bytes 4194304 | tf_op jit(solution)/shard_map/all_to_all | solution.py:134
  179.5 11.4 %copy.36 = bf16[8192,512]{0,1:T(8,128)(2,1)} copy(bf16[8192,512]{1,0:T(8,128)(2,1)} %get-tuple-element.14) | data formatting | bytes 16777216 | tf_op jit(solution)/shard_map/split | solution.py:90
  190.9 9.5 %fusion.16 = f32[4,512,128]{1,2,0:T(8,128)S(1)} fusion(bf16[8192,4,128]{0,2,1:T(8,128)(2,1)} %bitcast.154, bf16[512,8192]{1,0:T(8,128)(2,1)} %param.8), kind=kOutput, calls=%fused_computation.26 | convolution fusion | flops 4294967296 | bytes 17825792 | tf_op jit(solution)/shard_map/rn,nkd->krd/dot_general | solution.py:98
  201.4 2.1 copy.37
  203.4 15.5 %all-to-all-done.1 = bf16[16,512,128]{2,1,0:T(8,128)(2,1)S(1)} async-done(((bf16[16,512,128]{2,1,0:T(8,128)(2,1)}), bf16[16,512,128]{2,1,0:T(8,128)(2,1)S(1)}, u32[]{:S(2)}, u32[]{:S(2)}) %all-to-all-start.1) | async-done | bytes 2097184 | tf_op jit(solution)/shard_map/all_to_all | solution.py:134
  219.0 2.8 broadcast_in_dim.13
  221.8 11.2 %all-to-all-start = ((bf16[16,512,128]{2,1,0:T(8,128)(2,1)}), bf16[16,512,128]{2,1,0:T(8,128)(2,1)}, u32[]{:S(2)}, u32[]{:S(2)}) async-start(bf16[16,512,128]{2,1,0:T(8,128)(2,1)} %bitcast.4), calls=%async_computation | async-start | bytes 4194304 | tf_op jit(solution)/shard_map/all_to_all | solution.py:133
  233.1 6.4 %copy.61 = bf16[256,8192]{1,0:T(8,128)(2,1)} copy(bf16[256,8192]{0,1:T(8,128)(2,1)} %bitcast.158) | data formatting | bytes 8388608 | tf_op jit(solution)/shard_map/dot_general | solution.py:118
  239.6 3.6 fusion.37
  245.1 2.1 fusion.14
  247.6 2.1 fusion.34
  249.7 2.2 gather_fusion.3
  251.9 22.3 %all-to-all-done = bf16[16,512,128]{2,1,0:T(8,128)(2,1)} async-done(((bf16[16,512,128]{2,1,0:T(8,128)(2,1)}), bf16[16,512,128]{2,1,0:T(8,128)(2,1)}, u32[]{:S(2)}, u32[]{:S(2)}) %all-to-all-start) | async-done | bytes 2097184 | tf_op jit(solution)/shard_map/all_to_all | solution.py:133
  274.2 2.5 gather_fusion
  276.7 2.6 fusion.78
  279.5 3.1 fusion.6
  282.9 2.5 fusion.25
  288.8 4.0 %convolution_convert_fusion = bf16[2,32,8192]{2,1,0:T(8,128)(2,1)} fusion(bf16[256,8192]{1,0:T(8,128)(2,1)} %param.15, bf16[1,32,256]{2,1,0:T(8,128)(2,1)S(1)} %stack.10, bf16[1,32,256]{2,1,0:T(8,128)(2,1)S(1)} %stack.9), kind=kOutput, calls=%fused_computation.10 | convolution fusion | flops 268976128 | bytes 5275648 | tf_op jit(solution)/shard_map/srk,kd->srd/dot_general | solution.py:169
  292.9 64.0 %reduce-scatter.2.cloned.1.call-done = bf16[2,32,512]{2,1,0:T(8,128)(2,1)} async-done(((bf16[2,32,8192]{2,1,0:T(8,128)(2,1)}), bf16[2,32,512]{2,1,0:T(8,128)(2,1)}) %reduce-scatter.2.cloned.1.call-update) | async-done | bytes 65552 | tf_op jit(solution)/shard_map/reduce_scatter | solution.py:172
  (66 shorter events, 10.8 us)
Async XLA Ops:
  6.5 233.1 %copy-start = (bf16[2,32,8192]{2,1,0:T(8,128)(2,1)S(1)}, bf16[2,32,8192]{2,1,0:T(8,128)(2,1)}, u32[]{:S(2)}) copy-start(bf16[2,32,8192]{2,1,0:T(8,128)(2,1)} %param.10) | copy-start | bytes 3145732
  6.5 132.6 %all-gather.2.cloned.1.call-start = ((), (), s32[]{:S(2)}) async-start(), calls=%async_computation.3 | async-start | bytes 17825792 | tf_op jit(solution)/shard_map/all_gather | solution.py:91
  172.1 5.8 %copy-start.2 = (s32[64]{0:T(128)S(1)}, s32[64]{0:T(128)}, u32[]{:S(2)}) copy-start(s32[64]{0:T(128)} %param.9) | copy-start | bytes 772
  174.2 44.8 %all-to-all-start.1 = ((bf16[16,512,128]{2,1,0:T(8,128)(2,1)}), bf16[16,512,128]{2,1,0:T(8,128)(2,1)S(1)}, u32[]{:S(2)}, u32[]{:S(2)}) async-start(bf16[16,512,128]{2,1,0:T(8,128)(2,1)} %bitcast.26), calls=%async_computation.1 | async-start | bytes 4194304 | tf_op jit(solution)/shard_map/all_to_all | solution.py:134
  221.8 52.4 %all-to-all-start = ((bf16[16,512,128]{2,1,0:T(8,128)(2,1)}), bf16[16,512,128]{2,1,0:T(8,128)(2,1)}, u32[]{:S(2)}, u32[]{:S(2)}) async-start(bf16[16,512,128]{2,1,0:T(8,128)(2,1)} %bitcast.4), calls=%async_computation | async-start | bytes 4194304 | tf_op jit(solution)/shard_map/all_to_all | solution.py:133
  233.0 123.8 %reduce-scatter.2.cloned.1.call-start = ((), (), s32[]{:S(2)}) async-start(), calls=%async_computation.4 | async-start | bytes 1114112 | tf_op jit(solution)/shard_map/reduce_scatter | solution.py:172
  239.5 4.0 %copy-start.3 = (s32[32]{0:T(128)S(1)}, s32[32]{0:T(128)}, u32[]{:S(2)}) copy-start(s32[32]{0:T(128)} %param.11) | copy-start | bytes 388
  279.5 3.5 copy-start.1
Sparse Core Ops, SparseCore 0:
  9.5 129.5 all-gather.1
  293.0 63.8 reduce-scatter.1
